TPU v7x, 32 devices: a whole 2x2x4 slice. The times are simulated.
32 devices in a mesh: seqa: 2 (over y), seqb: 4 (over z), tp: 4 (over x, core).
Axes of the slice: x: 2, y: 2, z: 4, core: 2. Of those that a mesh axis runs over, the one named last changes fastest.
Arguments:
- queries: bfloat16 [4096, 1024], P(('seqa', 'seqb'), 'tp'), may hold values from -6 to 6
- key_rows: bfloat16 [4096, 1024], P(('seqa', 'seqb'), 'tp'), may hold values from -6 to 6
- value_rows: bfloat16 [4096, 1024], P(('seqa', 'seqb'), 'tp'), may hold values from -6 to 6
- out_grad: bfloat16 [4096, 2048], P(('seqa', 'seqb'), 'tp'), may hold values from -6 to 6
- out_weight: bfloat16 [1024, 2048], P('tp'), may hold values from -0.1875 to 0.1875
- level_codes: int32 [4096, 160], P(('seqa', 'seqb'), 'tp'), may hold values from 0 to 7
Outputs:
- query_grad: bfloat16 [4096, 1024], P(('seqa', 'seqb'), 'tp')
- key_grad: bfloat16 [4096, 1024], P(('seqa', 'seqb'), 'tp')
- value_grad: bfloat16 [4096, 1024], P(('seqa', 'seqb'), 'tp')
All inputs are finite; a program needn't handle non-finite values.
Results may differ from a plain program's by a relative error of at most 0.0062.
Values may be sent and summed in bfloat16 or wider, within the bound.
A program may use at most 64 MiB of HBM per device.

v0:
```python
import math
import jax
import jax.numpy as jnp
from jax import lax
from jax.sharding import PartitionSpec as P

HEAD_DIM = 128


def swapped(x, axis, distance):
    return lax.ppermute(x, axis, [(i, i ^ 1 << distance) for i in range(lax.axis_size(axis))])


def per_device(queries, key_rows, value_rows, out_grad, out_weight, level_codes):
    shard_rows = queries.shape[0]
    head_count = out_weight.shape[0] // HEAD_DIM
    total_tokens = shard_rows * lax.axis_size(("seqa", "seqb"))
    scale_factor = 1.0 / math.sqrt(HEAD_DIM * total_tokens)
    head_grad = lax.dot_general(
        lax.all_gather(out_grad, "tp", axis=1, tiled=True),
        out_weight,
        (((1,), (1,)), ((), ())),
        preferred_element_type=jnp.float32,
    ).astype(jnp.bfloat16)
    level_weight = ((1 + level_codes).astype(jnp.float32) / 8.0).reshape(shard_rows, head_count, -1)
    shape_three = (shard_rows, head_count, HEAD_DIM)
    query_heads = queries.reshape(shape_three)
    key_head_matrix = key_rows.reshape(shape_three)
    value_head_matrix = value_rows.reshape(shape_three)
    grad_heads = head_grad.reshape(shape_three)
    level_top = shard_rows.bit_length() - 1
    span = min(shard_rows, 512)
    key_intra = jnp.zeros(shape_three, jnp.float32)
    value_intra = jnp.zeros(shape_three, jnp.float32)
    query_pos = jnp.arange(0, span, dtype=jnp.int32)[:, None]
    source_pos = jnp.arange(span, dtype=jnp.int32)[None, :]
    differ = jnp.bitwise_xor(query_pos, source_pos)
    level_map = jnp.zeros(differ.shape, jnp.int32)
    for bit_index in range(level_top):
        level_map = level_map + (differ >= 2**bit_index).astype(jnp.int32)
    causal = source_pos <= query_pos
    weight = jnp.zeros((head_count, span, span), jnp.float32)
    for level_index in range(level_top + 1):
        select = ((level_map == level_index) & causal).astype(jnp.float32)
        weight = weight + level_weight[:, :, level_index].T[:, :, None] * select[None]
    weight = weight * scale_factor
    scores = jnp.einsum(
        "thk,shk->hts", query_heads, key_head_matrix, preferred_element_type=jnp.float32
    )
    probs = (weight * scores).astype(jnp.bfloat16)
    dscore = jnp.einsum(
        "thv,shv->hts", grad_heads, value_head_matrix, preferred_element_type=jnp.float32
    )
    grad_mat = (weight * dscore).astype(jnp.bfloat16)
    query_parts = jnp.einsum(
        "hts,shk->thk", grad_mat, key_head_matrix, preferred_element_type=jnp.float32
    )
    key_intra = key_intra.at[:span].add(
        jnp.einsum("hts,thk->shk", grad_mat, query_heads, preferred_element_type=jnp.float32)
    )
    value_intra = value_intra.at[:span].add(
        jnp.einsum("hts,thv->shv", probs, grad_heads, preferred_element_type=jnp.float32)
    )
    carried_state = jnp.einsum(
        "ags,agr->gsr", key_head_matrix, value_head_matrix, preferred_element_type=jnp.float32
    )
    level_count = lax.axis_size(("seqa", "seqb")).bit_length() - 1
    device_index = lax.axis_index(("seqa", "seqb"))
    inter_weight = level_weight[:, :, level_top + 1 : level_top + 1 + level_count]
    scaled = (inter_weight[..., None] * grad_heads.astype(jnp.float32)[:, :, None, :]).astype(
        jnp.bfloat16
    )
    level_adjoint = scale_factor * jnp.einsum(
        "thk,thlv->lhkv", query_heads, scaled, preferred_element_type=jnp.float32
    )
    half_selector = [
        (device_index >> bit_index & 1).astype(jnp.float32) for bit_index in range(level_count)
    ]
    state_list = []
    total_adjoint = jnp.zeros(carried_state.shape, jnp.float32)
    for bit_index in range(level_count):
        upper = half_selector[bit_index]
        outgoing = upper * level_adjoint[bit_index] + (1.0 - upper) * carried_state
        received = swapped(outgoing, ("seqa", "seqb"), bit_index)
        for lower in range(bit_index):
            received = received + swapped(received, ("seqa", "seqb"), lower)
        state_list.append(received * upper)
        total_adjoint = total_adjoint + received * (1.0 - upper)
    level_states = jnp.stack(state_list, 0).astype(jnp.bfloat16)
    level_out = jnp.einsum(
        "thv,lhkv->thlk", grad_heads, level_states, preferred_element_type=jnp.float32
    )
    inter_sum = jnp.sum(inter_weight[..., None] * level_out, axis=2)
    adjoint_bfloat = total_adjoint.astype(jnp.bfloat16)
    query_grad = (query_parts + scale_factor * inter_sum).astype(jnp.bfloat16)
    key_grad = (
        key_intra
        + jnp.einsum(
            "ybe,bpe->ybp", value_head_matrix, adjoint_bfloat, preferred_element_type=jnp.float32
        )
    ).astype(jnp.bfloat16)
    value_grad = (
        value_intra
        + jnp.einsum(
            "mix,ixy->miy", key_head_matrix, adjoint_bfloat, preferred_element_type=jnp.float32
        )
    ).astype(jnp.bfloat16)
    flat = (shard_rows, head_count * HEAD_DIM)
    return (query_grad.reshape(flat), key_grad.reshape(flat), value_grad.reshape(flat))


def solution(mesh):
    placed = (
        P(("seqa", "seqb"), "tp"),
        P(("seqa", "seqb"), "tp"),
        P(("seqa", "seqb"), "tp"),
        P(("seqa", "seqb"), "tp"),
        P("tp", None),
        P(("seqa", "seqb"), "tp"),
    )
    return jax.shard_map(
        per_device,
        mesh=mesh,
        in_specs=placed,
        out_specs=(P(("seqa", "seqb"), "tp"), P(("seqa", "seqb"), "tp"), P(("seqa", "seqb"), "tp")),
        check_vma=False,
    )
```

profile of v0, /device:TPU:0, one launch (start us, length us, event | category | flops | bytes accessed | tf_op | source)
XLA Modules:
  0.0 76.9 jit_solution(2021714095588899248)
XLA Ops:
  7.2 0.0 copy-start
  7.2 0.0 all-gather.2.cloned.1.call-start
  7.2 0.7 all-gather.2.cloned.1.call-update
  7.9 0.9 %convert_multiply_fusion = f32[512,40]{0,1:T(8,128)S(1)} fusion(s32[512,40]{0,1:T(8,128)} %param.19), kind=kLoop, calls=%fused_computation.91 | loop fusion | flops 61440 | bytes 163840 | tf_op jit(solution)/shard_map/div | solution.py:25
  8.9 1.8 %fusion.35 = (f32[512,512]{1,0:T(8,128)}, f32[512,512]{1,0:T(8,128)}) fusion(), kind=kLoop, calls=%fused_computation.49 | loop fusion | flops 8912896 | bytes 2097152 | tf_op jit(solution)/shard_map/convert_element_type | solution.py:44
  10.6 1.9 %fusion.33 = (f32[512,512]{1,0:T(8,128)}, f32[512,512]{1,0:T(8,128)}) fusion(), kind=kLoop, calls=%fused_computation.47 | loop fusion | flops 8912896 | bytes 2097152 | tf_op jit(solution)/shard_map/convert_element_type | solution.py:44
  12.5 1.8 %fusion.31 = (f32[512,512]{1,0:T(8,128)}, f32[512,512]{1,0:T(8,128)}) fusion(), kind=kLoop, calls=%fused_computation.45 | loop fusion | flops 8912896 | bytes 2097152 | tf_op jit(solution)/shard_map/convert_element_type | solution.py:44
  14.4 1.8 %fusion.29 = (f32[512,512]{1,0:T(8,128)}, f32[512,512]{1,0:T(8,128)}) fusion(), kind=kLoop, calls=%fused_computation.43 | loop fusion | flops 8912896 | bytes 2097152 | tf_op jit(solution)/shard_map/convert_element_type | solution.py:44
  16.2 1.8 %fusion.27 = (f32[512,512]{1,0:T(8,128)}, f32[512,512]{1,0:T(8,128)}) fusion(), kind=kLoop, calls=%fused_computation.41 | loop fusion | flops 8912896 | bytes 2097152 | tf_op jit(solution)/shard_map/convert_element_type | solution.py:44
  18.0 16.8 %all-gather.2.cloned.1.call-done = bf16[512,2048]{1,0:T(8,128)(2,1)} async-done(((bf16[512,512]{1,0:T(8,128)(2,1)}), bf16[512,2048]{1,0:T(8,128)(2,1)}) %all-gather.2.cloned.1.call-update) | async-done | bytes 2097168 | tf_op jit(solution)/shard_map/all_gather | solution.py:20
  34.9 0.0 copy-done
  34.9 0.0 copy-start.7
  34.9 0.0 copy-start.8
  34.9 0.0 copy-start.9
  34.9 2.5 %convolution_convert_fusion = bf16[512,256]{0,1:T(8,128)(2,1)S(1)} fusion(bf16[512,2048]{1,0:T(8,128)(2,1)} %all-gather.2.cloned.1.call-done, bf16[256,2048]{1,0:T(8,128)(2,1)S(1)} %copy-done), kind=kOutput, calls=%fused_computation.15 | convolution fusion | flops 537001984 | bytes 3407872 | tf_op jit(solution)/shard_map/dot_general | solution.py:19
  37.4 0.0 copy-start.2
  37.4 0.0 copy-start.3
  37.4 0.0 copy-start.4
  37.4 0.1 convert_element_type.608
  37.5 0.0 copy-done.16
  37.5 0.4 fusion.7
  37.9 0.0 copy-done.13
  37.9 0.0 copy-done.10
  37.9 0.9 %fusion.71 = (f32[2,128,128]{1,2,0:T(8,128)}, f32[2,128,128]{1,2,0:T(8,128)S(1)}, f32[2,128,128]{1,2,0:T(8,128)S(1)}) fusion(f32[3,2,128,128]{2,3,0,1:T(8,128)S(1)} %fusion.7, f32[]{:T(128)S(6)} %sub.12, f32[]{:T(128)S(6)} %convert_element_type.607, f32[]{:T(128)S(6)} %sub.14, f32[]{:T(128)S(6)} %convert_element_type.611, f32[]{:T(128)S(6)} %sub.13, ...), kind=kOutput, calls=%fused_computation.86 | convolution fusion | flops 33849344 | bytes 1310744 | tf_op jit(solution)/shard_map/ags,agr->gsr/dot_general | solution.py:64
  38.9 1.5 %collective-permute-start.3 = (f32[2,128,128]{1,2,0:T(8,128)S(1)}, f32[2,128,128]{1,2,0:T(8,128)S(1)}, u32[]{:S(2)}, u32[]{:S(2)}) collective-permute-start(f32[2,128,128]{1,2,0:T(8,128)S(1)} %get-tuple-element.50), channel_id=1, source_target_pairs={{0,16},{4,20},{8,24},{12,28},{16,0},{20,4},{24,8},{28,12},{1,17},{... | collective-permute-start | bytes 393224 | tf_op jit(solution)/shard_map/ppermute | solution.py:11
  40.3 0.0 copy-done.5
  40.3 0.0 copy-done.6
  40.3 0.0 copy-done.7
  40.3 0.0 copy-done.8
  40.3 0.0 copy-done.9
  40.3 0.0 copy-done.2
  40.4 0.0 copy-done.3
  40.4 0.0 copy-done.4
  40.4 0.0 copy-start.14
  40.4 3.5 %add_multiply_fusion = f32[2,512,512]{2,1,0:T(8,128)S(1)} fusion(f32[512,512]{1,0:T(8,128)S(1)} %copy-done.3, f32[2,512]{1,0:T(2,128)S(1)} %get-tuple-element.66, f32[512,512]{1,0:T(8,128)S(1)} %copy-done.2, f32[2,512]{1,0:T(2,128)S(1)} %get-tuple-element.67, f32[512,512]{1,0:T(8,128)S(1)} %copy-done.5, f32[2,512]{1,0:T(2,128)S(1)} %get-tuple-element.68, ...), kind=kLoop, calls=%fused_computation.2 | loop fusion | flops 10485760 | bytes 12623872 | tf_op jit(solution)/shard_map/mul | solution.py:46
  43.9 2.5 %collective-permute-start.1 = (f32[2,128,128]{1,2,0:T(8,128)S(1)}, f32[2,128,128]{1,2,0:T(8,128)}, u32[]{:S(2)}, u32[]{:S(2)}) collective-permute-start(f32[2,128,128]{1,2,0:T(8,128)S(1)} %get-tuple-element.51), channel_id=1, source_target_pairs={{0,8},{4,12},{8,0},{12,4},{16,24},{20,28},{24,16},{28,20},{1,9},{5... | collective-permute-start | bytes 393224 | tf_op jit(solution)/shard_map/ppermute | solution.py:11
  46.4 0.0 collective-permute-done.3
  46.4 1.5 %collective-permute-start.4 = (f32[2,128,128]{1,2,0:T(8,128)S(1)}, f32[2,128,128]{1,2,0:T(8,128)S(1)}, u32[]{:S(2)}, u32[]{:S(2)}) collective-permute-start(f32[2,128,128]{1,2,0:T(8,128)S(1)} %collective-permute-done.3), channel_id=1, source_target_pairs={{0,4},{4,0},{8,12},{12,8},{16,20},{20,16},{24,28},{28,24},{1,5},{5... | collective-permute-start | bytes 393224 | tf_op jit(solution)/shard_map/ppermute | solution.py:11
  47.9 0.0 copy-done.14
  47.9 1.5 %multiply_convert_fusion.1 = bf16[2,512,512]{2,1,0:T(8,128)(2,1)} fusion(f32[2,512,512]{2,1,0:T(8,128)S(1)} %add_multiply_fusion, bf16[512,2,128]{0,2,1:T(8,128)(2,1)S(1)} %bitcast.185, bf16[512,256]{1,0:T(8,128)(2,1)S(1)} %copy-done.14), kind=kOutput, calls=%fused_computation.1 | convolution fusion | flops 135266304 | bytes 3670016 | tf_op jit(solution)/shard_map/thv,shv->hts/dot_general | solution.py:51
  49.4 0.5 collective-permute-start
  49.9 3.4 %collective-permute-done.1 = f32[2,128,128]{1,2,0:T(8,128)} collective-permute-done((f32[2,128,128]{1,2,0:T(8,128)S(1)}, f32[2,128,128]{1,2,0:T(8,128)}, u32[]{:S(2)}, u32[]{:S(2)}) %collective-permute-start.1) | collective-permute-done | bytes 131104 | tf_op jit(solution)/shard_map/ppermute | solution.py:11
  53.3 0.3 collective-permute-start.2
  53.6 0.2 collective-permute-done.4
  53.8 0.0 copy-start.17
  53.8 3.4 %collective-permute-start.5 = (f32[2,128,128]{1,2,0:T(8,128)S(1)}, f32[2,128,128]{1,2,0:T(8,128)}, u32[]{:S(2)}, u32[]{:S(2)}) collective-permute-start(f32[2,128,128]{1,2,0:T(8,128)S(1)} %add.524), channel_id=1, source_target_pairs={{0,8},{4,12},{8,0},{12,4},{16,24},{20,28},{24,16},{28,20},{1,9},{5... | collective-permute-start | bytes 393224 | tf_op jit(solution)/shard_map/ppermute | solution.py:11
  57.2 2.4 %fusion.1 = f32[2,128,512]{2,1,0:T(8,128)} fusion(bf16[512,2,128]{0,2,1:T(8,128)(2,1)S(1)} %bitcast.186, f32[2,512,512]{2,1,0:T(8,128)S(1)} %add_multiply_fusion, bf16[512,256]{1,0:T(8,128)(2,1)} %param.14, bf16[512,256]{1,0:T(8,128)(2,1)} %param.15), kind=kOutput, calls=%fused_computation.6 | convolution fusion | flops 269484032 | bytes 3407872 | tf_op jit(solution)/shard_map/hts,thv->shv/dot_general | solution.py:62
  59.6 0.0 collective-permute-done
  59.6 2.0 %collective-permute-done.2 = f32[2,128,128]{1,2,0:T(8,128)} collective-permute-done((f32[2,128,128]{1,2,0:T(8,128)}, f32[2,128,128]{1,2,0:T(8,128)}, u32[]{:S(2)}, u32[]{:S(2)}) %collective-permute-start.2) | collective-permute-done | bytes 131104 | tf_op jit(solution)/shard_map/ppermute | solution.py:11
  61.7 0.0 copy-done.17
  61.7 1.9 %collective-permute-done.5 = f32[2,128,128]{1,2,0:T(8,128)} collective-permute-done((f32[2,128,128]{1,2,0:T(8,128)S(1)}, f32[2,128,128]{1,2,0:T(8,128)}, u32[]{:S(2)}, u32[]{:S(2)}) %collective-permute-start.5) | collective-permute-done | bytes 131104 | tf_op jit(solution)/shard_map/ppermute | solution.py:11
  63.5 1.2 %add_convert_fusion = (bf16[2,128,128]{1,2,0:T(8,128)(2,1)S(1)}, bf16[1,2,128,128]{2,3,1,0:T(8,128)(2,1)S(1)}, bf16[1,2,128,128]{2,3,1,0:T(8,128)(2,1)S(1)}, bf16[1,2,128,128]{2,3,1,0:T(8,128)(2,1)S(1)}) fusion(f32[2,128,128]{1,2,0:T(8,128)} %collective-permute-done, f32[]{:T(128)S(6)} %sub.14, f32[]{:T(128)S(6)} %sub.13, f32[]{:T(128)S(6)} %sub.12, ...), kind=kLoop, calls=%fused_computation.87 | loop fusion | flops 458752 | bytes 917528 | tf_op jit(solution)/shard_map/convert_element_type | solution.py:94
  64.8 0.0 copy-start.15
  64.8 0.4 fusion
  65.2 0.0 copy-done.1
  65.2 0.0 copy-done.11
  65.2 0.5 fusion.4
  65.7 0.0 copy-start.12
  65.7 0.8 %copy.56 = bf16[512,256]{1,0:T(8,128)(2,1)} copy(bf16[512,256]{0,1:T(8,128)(2,1)S(1)} %bitcast.190) | data formatting | bytes 524288
  66.6 0.3 convolution_bitcast_fusion.1
  66.8 1.3 %fusion.5 = bf16[512,2,128]{0,2,1:T(8,128)(2,1)S(1)} fusion(f32[512,2,128]{0,2,1:T(8,128)S(1)} %convolution_bitcast_fusion.1, bf16[2,512,512]{2,1,0:T(8,128)(2,1)S(1)} %copy-done.1, bf16[512,256]{1,0:T(8,128)(2,1)} %param.14), kind=kOutput, calls=%fused_computation.14 | convolution fusion | flops 134479872 | bytes 2097152 | tf_op jit(solution)/shard_map/hts,thk->shk/dot_general | solution.py:59
  68.1 0.8 %copy.57 = bf16[512,256]{1,0:T(8,128)(2,1)} copy(bf16[512,256]{0,1:T(8,128)(2,1)S(1)} %bitcast.189) | data formatting | bytes 524288
  69.0 0.2 fusion.6
  69.2 0.8 %copy.58 = bf16[512,256]{1,0:T(8,128)(2,1)} copy(bf16[512,256]{0,1:T(8,128)(2,1)S(1)} %bitcast.188) | data formatting | bytes 524288
  (18 shorter events, 0.1 us)
Async XLA Ops:
  7.2 27.7 %copy-start = (bf16[256,2048]{1,0:T(8,128)(2,1)S(1)}, bf16[256,2048]{1,0:T(8,128)(2,1)}, u32[]{:S(2)}) copy-start(bf16[256,2048]{1,0:T(8,128)(2,1)} %param.18) | copy-start | bytes 3145732
  7.2 27.7 %all-gather.2.cloned.1.call-start = ((), (), s32[]{:S(2)}) async-start(), calls=%async_computation | async-start | bytes 2621440 | tf_op jit(solution)/shard_map/all_gather | solution.py:20
  16.2 21.3 %copy-start.16 = (bf16[512,256]{1,0:T(8,128)(2,1)S(1)}, bf16[512,256]{1,0:T(8,128)(2,1)}, u32[]{:S(2)}) copy-start(bf16[512,256]{1,0:T(8,128)(2,1)} %param.14) | copy-start | bytes 786436
  16.2 21.7 %copy-start.13 = (bf16[512,256]{1,0:T(8,128)(2,1)S(1)}, bf16[512,256]{1,0:T(8,128)(2,1)}, u32[]{:S(2)}) copy-start(bf16[512,256]{1,0:T(8,128)(2,1)} %param.16) | copy-start | bytes 786436
  34.9 3.0 %copy-start.10 = (bf16[512,256]{1,0:T(8,128)(2,1)S(1)}, bf16[512,256]{1,0:T(8,128)(2,1)}, u32[]{:S(2)}) copy-start(bf16[512,256]{1,0:T(8,128)(2,1)} %param.15) | copy-start | bytes 786436
  34.9 5.5 %copy-start.5 = (f32[512,512]{1,0:T(8,128)S(1)}, f32[512,512]{1,0:T(8,128)}, u32[]{:S(2)}) copy-start(f32[512,512]{1,0:T(8,128)} %get-tuple-element.83) | copy-start | bytes 3145732
  34.9 5.5 %copy-start.6 = (f32[512,512]{1,0:T(8,128)S(1)}, f32[512,512]{1,0:T(8,128)}, u32[]{:S(2)}) copy-start(f32[512,512]{1,0:T(8,128)} %get-tuple-element.80) | copy-start | bytes 3145732
  34.9 5.5 %copy-start.7 = (f32[512,512]{1,0:T(8,128)S(1)}, f32[512,512]{1,0:T(8,128)}, u32[]{:S(2)}) copy-start(f32[512,512]{1,0:T(8,128)} %get-tuple-element.81) | copy-start | bytes 3145732
  34.9 5.4 %copy-start.8 = (f32[512,512]{1,0:T(8,128)S(1)}, f32[512,512]{1,0:T(8,128)}, u32[]{:S(2)}) copy-start(f32[512,512]{1,0:T(8,128)} %get-tuple-element.78) | copy-start | bytes 3145732
  34.9 5.4 %copy-start.9 = (f32[512,512]{1,0:T(8,128)S(1)}, f32[512,512]{1,0:T(8,128)}, u32[]{:S(2)}) copy-start(f32[512,512]{1,0:T(8,128)} %get-tuple-element.79) | copy-start | bytes 3145732
  37.4 2.9 %copy-start.2 = (f32[512,512]{1,0:T(8,128)S(1)}, f32[512,512]{1,0:T(8,128)}, u32[]{:S(2)}) copy-start(f32[512,512]{1,0:T(8,128)} %get-tuple-element.84) | copy-start | bytes 3145732
  37.4 2.9 %copy-start.3 = (f32[512,512]{1,0:T(8,128)S(1)}, f32[512,512]{1,0:T(8,128)}, u32[]{:S(2)}) copy-start(f32[512,512]{1,0:T(8,128)} %get-tuple-element.85) | copy-start | bytes 3145732
  37.4 2.9 %copy-start.4 = (f32[512,512]{1,0:T(8,128)S(1)}, f32[512,512]{1,0:T(8,128)}, u32[]{:S(2)}) copy-start(f32[512,512]{1,0:T(8,128)} %get-tuple-element.82) | copy-start | bytes 3145732
  38.9 7.5 %collective-permute-start.3 = (f32[2,128,128]{1,2,0:T(8,128)S(1)}, f32[2,128,128]{1,2,0:T(8,128)S(1)}, u32[]{:S(2)}, u32[]{:S(2)}) collective-permute-start(f32[2,128,128]{1,2,0:T(8,128)S(1)} %get-tuple-element.50), channel_id=1, source_target_pairs={{0,16},{4,20},{8,24},{12,28},{16,0},{20,4},{24,8},{28,12},{1,17},{... | collective-permute-start | bytes 393224 | tf_op jit(solution)/shard_map/ppermute | solution.py:11
  40.4 7.5 %copy-start.14 = (bf16[512,256]{1,0:T(8,128)(2,1)S(1)}, bf16[512,256]{1,0:T(8,128)(2,1)}, u32[]{:S(2)}) copy-start(bf16[512,256]{1,0:T(8,128)(2,1)} %param.16) | copy-start | bytes 786436
  43.9 9.3 %collective-permute-start.1 = (f32[2,128,128]{1,2,0:T(8,128)S(1)}, f32[2,128,128]{1,2,0:T(8,128)}, u32[]{:S(2)}, u32[]{:S(2)}) collective-permute-start(f32[2,128,128]{1,2,0:T(8,128)S(1)} %get-tuple-element.51), channel_id=1, source_target_pairs={{0,8},{4,12},{8,0},{12,4},{16,24},{20,28},{24,16},{28,20},{1,9},{5... | collective-permute-start | bytes 393224 | tf_op jit(solution)/shard_map/ppermute | solution.py:11
  46.4 7.4 %collective-permute-start.4 = (f32[2,128,128]{1,2,0:T(8,128)S(1)}, f32[2,128,128]{1,2,0:T(8,128)S(1)}, u32[]{:S(2)}, u32[]{:S(2)}) collective-permute-start(f32[2,128,128]{1,2,0:T(8,128)S(1)} %collective-permute-done.3), channel_id=1, source_target_pairs={{0,4},{4,0},{8,12},{12,8},{16,20},{20,16},{24,28},{28,24},{1,5},{5... | collective-permute-start | bytes 393224 | tf_op jit(solution)/shard_map/ppermute | solution.py:11
  49.4 10.3 %collective-permute-start = (f32[2,128,128]{1,2,0:T(8,128)}, f32[2,128,128]{1,2,0:T(8,128)}, u32[]{:S(2)}, u32[]{:S(2)}) collective-permute-start(f32[2,128,128]{1,2,0:T(8,128)} %get-tuple-element.49), channel_id=1, source_target_pairs={{0,4},{4,0},{8,12},{12,8},{16,20},{20,16},{24,28},{28,24},{1,5},{5... | collective-permute-start | bytes 393224 | tf_op jit(solution)/shard_map/ppermute | solution.py:11
  53.3 8.4 %collective-permute-start.2 = (f32[2,128,128]{1,2,0:T(8,128)}, f32[2,128,128]{1,2,0:T(8,128)}, u32[]{:S(2)}, u32[]{:S(2)}) collective-permute-start(f32[2,128,128]{1,2,0:T(8,128)} %collective-permute-done.1), channel_id=1, source_target_pairs={{0,4},{4,0},{8,12},{12,8},{16,20},{20,16},{24,28},{28,24},{1,5},{5... | collective-permute-start | bytes 393224 | tf_op jit(solution)/shard_map/ppermute | solution.py:11
  53.8 7.9 %copy-start.17 = (f32[2,128,128]{1,2,0:T(8,128)}, f32[2,128,128]{1,2,0:T(8,128)S(1)}, u32[]{:S(2)}) copy-start(f32[2,128,128]{1,2,0:T(8,128)S(1)} %add.524) | copy-start | bytes 393220
  53.8 9.7 %collective-permute-start.5 = (f32[2,128,128]{1,2,0:T(8,128)S(1)}, f32[2,128,128]{1,2,0:T(8,128)}, u32[]{:S(2)}, u32[]{:S(2)}) collective-permute-start(f32[2,128,128]{1,2,0:T(8,128)S(1)} %add.524), channel_id=1, source_target_pairs={{0,8},{4,12},{8,0},{12,4},{16,24},{20,28},{24,16},{28,20},{1,9},{5... | collective-permute-start | bytes 393224 | tf_op jit(solution)/shard_map/ppermute | solution.py:11
  59.6 5.6 %copy-start.1 = (bf16[2,512,512]{2,1,0:T(8,128)(2,1)S(1)}, bf16[2,512,512]{2,1,0:T(8,128)(2,1)}, u32[]{:S(2)}) copy-start(bf16[2,512,512]{2,1,0:T(8,128)(2,1)} %multiply_convert_fusion.1) | copy-start | bytes 3145732
  59.6 5.6 %copy-start.11 = (bf16[512,256]{1,0:T(8,128)(2,1)S(1)}, bf16[512,256]{1,0:T(8,128)(2,1)}, u32[]{:S(2)}) copy-start(bf16[512,256]{1,0:T(8,128)(2,1)} %param.15) | copy-start | bytes 786436
  64.8 1.8 %copy-start.15 = (bf16[512,256]{1,0:T(8,128)(2,1)S(1)}, bf16[512,256]{1,0:T(8,128)(2,1)}, u32[]{:S(2)}) copy-start(bf16[512,256]{1,0:T(8,128)(2,1)} %param.16) | copy-start | bytes 786436
  65.7 3.3 %copy-start.12 = (f32[2,128,512]{2,1,0:T(8,128)S(1)}, f32[2,128,512]{2,1,0:T(8,128)}, u32[]{:S(2)}) copy-start(f32[2,128,512]{2,1,0:T(8,128)} %fusion.1) | copy-start | bytes 1572868
Sparse Core Ops, SparseCore 0:
  9.5 25.2 all-gather.1
where the time goes:
time: 77.2 us; the launch traced here: 76.9 us
  waiting for transfers between devices  25 us (32%)
  other arithmetic  14.8 us (19%)
  between operations  14.4 us (19%)
  matrix products  10.4 us (13%)
  starting transfers between devices  9.74 us (13%)
  local copies, waits for them, and re-layouts  2.68 us (3%)
    all_gather x1, waiting for transfers between devices, per_device(): lax.all_gather(out_grad, 'tp', axis=1, tiled=True)  16.8 us
    ppermute x6, starting transfers between devices, swapped(): lax.ppermute(x, axis, [(i, i ^ 1 << distance) for i in range(lax.axis_siz...  9.7 us
    convert_element_type x5, other arithmetic, per_device(): select = ((level_map == level_index) & causal).astype(jnp.float32)  9.07 us
    ppermute x6, waiting for transfers between devices, swapped(): lax.ppermute(x, axis, [(i, i ^ 1 << distance) for i in range(lax.axis_siz...  7.45 us
    mul x1, other arithmetic, per_device(): weight = weight * scale_factor  3.52 us
    unnamed x39, local copies, waits for them, and re-layouts  2.61 us
    dot_general x1, matrix products, per_device(): lax.dot_general(lax.all_gather(out_grad, 'tp', axis=1, tiled=True), out_w...  2.49 us
    dot_general x1, matrix products, per_device(): jnp.einsum('hts,thv->shv', probs, grad_heads, preferred_element_type=jnp....  2.4 us
  transfers between devices with their start and end apart: 7, of which 5 were waited for; matrix products, arithmetic and copies ran while one was open for 23% of the time, Pallas kernels for 0%

commit v1 on v0

--- a/solution.py
+++ b/solution.py
@@ -5,6 +5,19 @@
 from jax.sharding import PartitionSpec as P
 
 HEAD_DIM = 128
+
+
+def gather_around(shard, axis, dim):
+    ways = lax.axis_size(axis)
+    up = [(d, (d + 1) % ways) for d in range(ways)]
+    down = [(d, (d - 1) % ways) for d in range(ways)]
+    earlier, later = ([shard], [shard])
+    for _ in range(ways // 2):
+        earlier.append(lax.ppermute(earlier[-1], axis, up))
+    for _ in range((ways - 1) // 2):
+        later.append(lax.ppermute(later[-1], axis, down))
+    line = jnp.concatenate([*earlier[::-1], *later[1:]], axis=dim)
+    return jnp.roll(line, (lax.axis_index(axis) - ways // 2) * shard.shape[dim], axis=dim)
 
 
 def swapped(x, axis, distance):
@@ -17,7 +30,7 @@
     total_tokens = shard_rows * lax.axis_size(("seqa", "seqb"))
     scale_factor = 1.0 / math.sqrt(HEAD_DIM * total_tokens)
     head_grad = lax.dot_general(
-        lax.all_gather(out_grad, "tp", axis=1, tiled=True),
+        gather_around(out_grad, "tp", 1),
         out_weight,
         (((1,), (1,)), ((), ())),
         preferred_element_type=jnp.float32,

time: 77.2 us -> 56 us (0.73)
  between operations: 14.4 us -> 1.04 us
  waiting for transfers between devices: 25 us -> 17.8 us
  starting transfers between devices: 9.74 us -> 15.7 us
  other arithmetic: 14.8 us -> 9.35 us
  matrix products: 10.4 us -> 8.66 us
    all_gather x1 -> x0, waiting for transfers between devices: 16.8 us -> none  [per_device(): lax.all_gather(out_grad, 'tp', axis=1, tiled=True)]
    ppermute x0 -> x3, waiting for transfers between devices: none -> 9.62 us  [the longest x2 9.61 us: gather_around(): earlier.append(lax.ppermute(earlier[-1], axis, up))]
    ppermute x0 -> x3, starting transfers between devices: none -> 5.08 us  [the longest x2 3.1 us: gather_around(): earlier.append(lax.ppermute(earlier[-1], axis, up))]
    convert_element_type x5, other arithmetic: 9.07 us -> 6.3 us  [per_device(): select = ((level_map == level_index) & causal).astype(jnp.float32)]
    dot_general x1, matrix products: 2.49 us -> 0.77 us  [per_device(): lax.dot_general(gather_around(out_grad, 'tp', 1), out_weight, (((1,), (1,...]
    mul x1, other arithmetic: 3.52 us -> 1.81 us  [per_device(): weight = weight * scale_factor]
    ppermute x6, starting transfers between devices: 9.7 us -> 10.7 us  [swapped(): lax.ppermute(x, axis, [(i, i ^ 1 << distance) for i in range(lax.axis_siz...]
    div x1, other arithmetic: 0.9 us -> 0.01 us  [per_device(): (1 + level_codes).astype(jnp.float32) / 8.0]
  transfers between devices with their start and end apart: 7 -> 9, of which waited for: 5 -> 6; matrix products, arithmetic and copies ran while one was open for 23% -> 22% of each run, Pallas kernels for 0% -> 0%
where the time goes in v1:
time: 56 us; the launch traced here: 55.8 us
  waiting for transfers between devices  17.8 us (32%)
  starting transfers between devices  15.7 us (28%)
  other arithmetic  9.35 us (17%)
  matrix products  8.66 us (15%)
  local copies, waits for them, and re-layouts  3.25 us (6%)
  between operations  1.04 us (2%)
    ppermute x6, starting transfers between devices, swapped(): lax.ppermute(x, axis, [(i, i ^ 1 << distance) for i in range(lax.axis_siz...  10.7 us
    ppermute x2, waiting for transfers between devices, gather_around(): earlier.append(lax.ppermute(earlier[-1], axis, up))  9.61 us
    ppermute x6, waiting for transfers between devices, swapped(): lax.ppermute(x, axis, [(i, i ^ 1 << distance) for i in range(lax.axis_siz...  8.18 us
    convert_element_type x5, other arithmetic, per_device(): select = ((level_map == level_index) & causal).astype(jnp.float32)  6.3 us
    unnamed x42, local copies, waits for them, and re-layouts  3.1 us
    ppermute x2, starting transfers between devices, gather_around(): earlier.append(lax.ppermute(earlier[-1], axis, up))  3.1 us
    dot_general x1, matrix products, per_device(): jnp.einsum('hts,thv->shv', probs, grad_heads, preferred_element_type=jnp....  2.4 us
    ppermute x1, starting transfers between devices, gather_around(): later.append(lax.ppermute(later[-1], axis, down))  1.98 us
  transfers between devices with their start and end apart: 9, of which 6 were waited for; matrix products, arithmetic and copies ran while one was open for 22% of the time, Pallas kernels for 0%

profile of v1, /device:TPU:0, one launch (start us, length us, event | category | flops | bytes accessed | tf_op | source)
XLA Modules:
  0.0 55.8 jit_solution(14474551424669789795)
XLA Ops:
  0.6 0.0 copy-start
  0.6 0.0 copy-start.15
  0.7 0.5 collective-permute-start
  1.2 2.0 %collective-permute-start.2 = (bf16[512,512]{1,0:T(8,128)(2,1)}, bf16[512,512]{1,0:T(8,128)(2,1)S(1)}, u32[]{:S(2)}, u32[]{:S(2)}) collective-permute-start(bf16[512,512]{1,0:T(8,128)(2,1)} %param.17), channel_id=1, source_target_pairs={{0,3},{1,0},{2,1},{3,2},{4,7},{5,4},{6,5},{7,6},{8,11},{9,8},{10,9... | collective-permute-start | bytes 1572872 | tf_op jit(solution)/shard_map/ppermute | solution.py:18
  3.2 1.8 %fusion.40 = (f32[512,512]{1,0:T(8,128)}, f32[512,512]{1,0:T(8,128)}) fusion(), kind=kLoop, calls=%fused_computation.51 | loop fusion | flops 8912896 | bytes 2097152 | tf_op jit(solution)/shard_map/convert_element_type | solution.py:57
  5.0 1.8 %fusion.38 = (f32[512,512]{1,0:T(8,128)}, f32[512,512]{1,0:T(8,128)}) fusion(), kind=kLoop, calls=%fused_computation.49 | loop fusion | flops 8912896 | bytes 2097152 | tf_op jit(solution)/shard_map/convert_element_type | solution.py:57
  6.8 0.0 copy-done.15
  6.9 1.8 %fusion.36 = (f32[512,512]{1,0:T(8,128)}, f32[512,512]{1,0:T(8,128)}) fusion(), kind=kLoop, calls=%fused_computation.47 | loop fusion | flops 8912896 | bytes 2097152 | tf_op jit(solution)/shard_map/convert_element_type | solution.py:57
  8.7 4.5 %collective-permute-done = bf16[512,512]{1,0:T(8,128)(2,1)S(1)} collective-permute-done((bf16[512,512]{1,0:T(8,128)(2,1)}, bf16[512,512]{1,0:T(8,128)(2,1)S(1)}, u32[]{:S(2)}, u32[]{:S(2)}) %collective-permute-start) | collective-permute-done | bytes 524320 | tf_op jit(solution)/shard_map/ppermute | solution.py:16
  13.2 2.6 %collective-permute-start.1 = (bf16[512,512]{1,0:T(8,128)(2,1)S(1)}, bf16[512,512]{1,0:T(8,128)(2,1)S(1)}, u32[]{:S(2)}, u32[]{:S(2)}) collective-permute-start(bf16[512,512]{1,0:T(8,128)(2,1)S(1)} %collective-permute-done), channel_id=1, source_target_pairs={{0,1},{1,2},{2,3},{3,0},{4,5},{5,6},{6,7},{7,4},{8,9},{9,10},{10,1... | collective-permute-start | bytes 1572872 | tf_op jit(solution)/shard_map/ppermute | solution.py:16
  15.8 0.5 fusion.34
  16.2 0.0 copy-start.10
  16.2 0.5 fusion.32
  16.7 5.1 %collective-permute-done.1 = bf16[512,512]{1,0:T(8,128)(2,1)S(1)} collective-permute-done((bf16[512,512]{1,0:T(8,128)(2,1)S(1)}, bf16[512,512]{1,0:T(8,128)(2,1)S(1)}, u32[]{:S(2)}, u32[]{:S(2)}) %collective-permute-start.1) | collective-permute-done | bytes 524320 | tf_op jit(solution)/shard_map/ppermute | solution.py:16
  21.8 0.1 constant_dynamic-update-slice_fusion.7
  21.9 0.1 constant_dynamic-update-slice_fusion.6
  22.0 0.0 copy-done.10
  22.0 0.1 constant_dynamic-update-slice_fusion.5
  22.1 0.0 collective-permute-done.2
  22.1 0.1 constant_dynamic-update-slice_fusion.4
  22.1 0.1 constant_dynamic-update-slice_fusion.3
  22.2 0.1 constant_dynamic-update-slice_fusion.2
  22.3 0.1 constant_dynamic-update-slice_fusion.1
  22.4 0.1 constant_dynamic-update-slice_fusion
  22.4 0.0 copy-done
  22.5 0.0 copy-start.14
  22.5 0.0 copy-start.8
  22.5 0.0 copy-start.12
  22.5 0.0 copy-start.5
  22.5 0.0 copy-start.6
  22.5 0.0 copy-start.7
  22.5 0.8 %fusion.9 = bf16[512,256]{0,1:T(8,128)(2,1)S(1)} fusion(bf16[256,2048]{1,0:T(8,128)(2,1)S(1)} %copy-done, bf16[512,4096]{1,0:T(8,128)(2,1)S(1)} %constant_dynamic-update-slice_fusion, s32[]{:T(128)S(6)} %select_n.14), kind=kOutput, calls=%fused_computation.18 | convolution fusion | flops 537001984 | bytes 3407876 | tf_op jit(solution)/shard_map/dot_general | solution.py:32
  23.3 0.0 copy-start.2
  23.3 0.0 copy-start.3
  23.3 0.1 convert_element_type.608
  23.4 0.0 copy-done.14
  23.4 0.4 fusion.12
  23.8 0.9 %fusion.76 = (f32[2,128,128]{1,2,0:T(8,128)}, f32[2,128,128]{1,2,0:T(8,128)S(1)}, f32[2,128,128]{1,2,0:T(8,128)S(1)}) fusion(f32[3,2,128,128]{2,3,0,1:T(8,128)S(1)} %fusion.12, f32[]{:T(128)S(6)} %sub.21, f32[]{:T(128)S(6)} %convert_element_type.607, f32[]{:T(128)S(6)} %sub.23, f32[]{:T(128)S(6)} %convert_element_type.611, f32[]{:T(128)S(6)} %sub.22, ...), kind=kOutput, calls=%fused_computation.88 | convolution fusion | flops 33849344 | bytes 1310744 | tf_op jit(solution)/shard_map/ags,agr->gsr/dot_general | solution.py:77
  24.8 3.1 %collective-permute-start.6 = (f32[2,128,128]{1,2,0:T(8,128)S(1)}, f32[2,128,128]{1,2,0:T(8,128)S(1)}, u32[]{:S(2)}, u32[]{:S(2)}) collective-permute-start(f32[2,128,128]{1,2,0:T(8,128)S(1)} %get-tuple-element.50), channel_id=1, source_target_pairs={{0,16},{4,20},{8,24},{12,28},{16,0},{20,4},{24,8},{28,12},{1,17},{... | collective-permute-start | bytes 393224 | tf_op jit(solution)/shard_map/ppermute | solution.py:24
  27.9 1.8 %add_multiply_fusion = f32[2,512,512]{2,1,0:T(8,128)S(1)} fusion(f32[512,512]{1,0:T(8,128)S(1)} %copy-done.3, f32[2,512]{1,0:T(2,128)S(1)} %get-tuple-element.66, f32[512,512]{1,0:T(8,128)S(1)} %copy-done.2, f32[2,512]{1,0:T(2,128)S(1)} %get-tuple-element.67, f32[512,512]{1,0:T(8,128)S(1)} %copy-done.5, f32[2,512]{1,0:T(2,128)S(1)} %get-tuple-element.68, ...), kind=kLoop, calls=%fused_computation.4 | loop fusion | flops 10485760 | bytes 12623872 | tf_op jit(solution)/shard_map/mul | solution.py:59
  29.8 2.7 %collective-permute-start.4 = (f32[2,128,128]{1,2,0:T(8,128)S(1)}, f32[2,128,128]{1,2,0:T(8,128)}, u32[]{:S(2)}, u32[]{:S(2)}) collective-permute-start(f32[2,128,128]{1,2,0:T(8,128)S(1)} %get-tuple-element.51), channel_id=1, source_target_pairs={{0,8},{4,12},{8,0},{12,4},{16,24},{20,28},{24,16},{28,20},{1,9},{5... | collective-permute-start | bytes 393224 | tf_op jit(solution)/shard_map/ppermute | solution.py:24
  32.4 0.0 collective-permute-done.6
  32.4 1.6 %collective-permute-start.7 = (f32[2,128,128]{1,2,0:T(8,128)S(1)}, f32[2,128,128]{1,2,0:T(8,128)S(1)}, u32[]{:S(2)}, u32[]{:S(2)}) collective-permute-start(f32[2,128,128]{1,2,0:T(8,128)S(1)} %collective-permute-done.6), channel_id=1, source_target_pairs={{0,4},{4,0},{8,12},{12,8},{16,20},{20,16},{24,28},{28,24},{1,5},{5... | collective-permute-start | bytes 393224 | tf_op jit(solution)/shard_map/ppermute | solution.py:24
  34.0 1.5 %multiply_convert_fusion.1 = bf16[2,512,512]{2,1,0:T(8,128)(2,1)} fusion(f32[2,512,512]{2,1,0:T(8,128)S(1)} %add_multiply_fusion, bf16[512,2,128]{0,2,1:T(8,128)(2,1)S(1)} %bitcast.184, bf16[512,256]{1,0:T(8,128)(2,1)S(1)} %copy-done.12), kind=kOutput, calls=%fused_computation.1 | convolution fusion | flops 135266304 | bytes 3670016 | tf_op jit(solution)/shard_map/thv,shv->hts/dot_general | solution.py:64
  35.5 0.4 collective-permute-start.3
  35.9 3.4 %collective-permute-done.4 = f32[2,128,128]{1,2,0:T(8,128)} collective-permute-done((f32[2,128,128]{1,2,0:T(8,128)S(1)}, f32[2,128,128]{1,2,0:T(8,128)}, u32[]{:S(2)}, u32[]{:S(2)}) %collective-permute-start.4) | collective-permute-done | bytes 131104 | tf_op jit(solution)/shard_map/ppermute | solution.py:24
  39.4 0.1 collective-permute-start.5
  39.5 0.9 %collective-permute-done.7 = f32[2,128,128]{1,2,0:T(8,128)S(1)} collective-permute-done((f32[2,128,128]{1,2,0:T(8,128)S(1)}, f32[2,128,128]{1,2,0:T(8,128)S(1)}, u32[]{:S(2)}, u32[]{:S(2)}) %collective-permute-start.7) | collective-permute-done | bytes 131104 | tf_op jit(solution)/shard_map/ppermute | solution.py:24
  40.3 2.8 %collective-permute-start.8 = (f32[2,128,128]{1,2,0:T(8,128)S(1)}, f32[2,128,128]{1,2,0:T(8,128)}, u32[]{:S(2)}, u32[]{:S(2)}) collective-permute-start(f32[2,128,128]{1,2,0:T(8,128)S(1)} %add.537), channel_id=1, source_target_pairs={{0,8},{4,12},{8,0},{12,4},{16,24},{20,28},{24,16},{28,20},{1,9},{5... | collective-permute-start | bytes 393224 | tf_op jit(solution)/shard_map/ppermute | solution.py:24
  43.1 2.4 %fusion.3 = f32[2,128,512]{2,1,0:T(8,128)} fusion(bf16[512,2,128]{0,2,1:T(8,128)(2,1)S(1)} %bitcast.185, f32[2,512,512]{2,1,0:T(8,128)S(1)} %add_multiply_fusion, bf16[512,256]{1,0:T(8,128)(2,1)} %param.14, bf16[512,256]{1,0:T(8,128)(2,1)} %param.15), kind=kOutput, calls=%fused_computation.8 | convolution fusion | flops 269484032 | bytes 3407872 | tf_op jit(solution)/shard_map/hts,thv->shv/dot_general | solution.py:75
  45.5 0.0 collective-permute-done.3
  45.5 2.5 %collective-permute-done.5 = f32[2,128,128]{1,2,0:T(8,128)} collective-permute-done((f32[2,128,128]{1,2,0:T(8,128)}, f32[2,128,128]{1,2,0:T(8,128)}, u32[]{:S(2)}, u32[]{:S(2)}) %collective-permute-start.5) | collective-permute-done | bytes 131104 | tf_op jit(solution)/shard_map/ppermute | solution.py:24
  48.0 1.4 %collective-permute-done.8 = f32[2,128,128]{1,2,0:T(8,128)} collective-permute-done((f32[2,128,128]{1,2,0:T(8,128)S(1)}, f32[2,128,128]{1,2,0:T(8,128)}, u32[]{:S(2)}, u32[]{:S(2)}) %collective-permute-start.8) | collective-permute-done | bytes 131104 | tf_op jit(solution)/shard_map/ppermute | solution.py:24
  49.4 1.2 %add_convert_fusion = (bf16[2,128,128]{1,2,0:T(8,128)(2,1)S(1)}, bf16[1,2,128,128]{2,3,1,0:T(8,128)(2,1)S(1)}, bf16[1,2,128,128]{2,3,1,0:T(8,128)(2,1)S(1)}, bf16[1,2,128,128]{2,3,1,0:T(8,128)(2,1)S(1)}) fusion(f32[2,128,128]{1,2,0:T(8,128)} %collective-permute-done.3, f32[]{:T(128)S(6)} %sub.23, f32[]{:T(128)S(6)} %sub.22, f32[]{:T(128)S(6)} %sub.21, ...), kind=kLoop, calls=%fused_computation.89 | loop fusion | flops 458752 | bytes 917528 | tf_op jit(solution)/shard_map/convert_element_type | solution.py:107
  50.6 0.0 copy-start.13
  50.6 0.4 fusion.2
  51.0 0.5 fusion.6
  51.5 0.8 %copy.56 = bf16[512,256]{1,0:T(8,128)(2,1)} copy(bf16[512,256]{0,1:T(8,128)(2,1)S(1)} %bitcast.189) | data formatting | bytes 524288
  52.4 0.0 copy-done.13
  52.4 0.3 convolution_bitcast_fusion.1
  52.6 1.3 %fusion.7 = bf16[512,2,128]{0,2,1:T(8,128)(2,1)S(1)} fusion(f32[512,2,128]{0,2,1:T(8,128)S(1)} %convolution_bitcast_fusion.1, bf16[2,512,512]{2,1,0:T(8,128)(2,1)S(1)} %copy-done.1, bf16[512,256]{1,0:T(8,128)(2,1)} %param.14), kind=kOutput, calls=%fused_computation.16 | convolution fusion | flops 134479872 | bytes 2097152 | tf_op jit(solution)/shard_map/hts,thk->shk/dot_general | solution.py:72
  53.9 0.8 %copy.57 = bf16[512,256]{1,0:T(8,128)(2,1)} copy(bf16[512,256]{0,1:T(8,128)(2,1)S(1)} %bitcast.188) | data formatting | bytes 524288
  54.8 0.2 fusion.8
  55.0 0.8 %copy.58 = bf16[512,256]{1,0:T(8,128)(2,1)} copy(bf16[512,256]{0,1:T(8,128)(2,1)S(1)} %bitcast.187) | data formatting | bytes 524288
  (25 shorter events, 0.1 us)
Async XLA Ops:
  0.6 21.8 %copy-start = (bf16[256,2048]{1,0:T(8,128)(2,1)S(1)}, bf16[256,2048]{1,0:T(8,128)(2,1)}, u32[]{:S(2)}) copy-start(bf16[256,2048]{1,0:T(8,128)(2,1)} %param.18) | copy-start | bytes 3145732
  0.6 6.1 %copy-start.15 = (s32[512,40]{0,1:T(8,128)S(1)}, s32[512,40]{0,1:T(8,128)}, u32[]{:S(2)}) copy-start(s32[512,40]{0,1:T(8,128)} %param.19) | copy-start | bytes 245764
  0.7 12.6 %collective-permute-start = (bf16[512,512]{1,0:T(8,128)(2,1)}, bf16[512,512]{1,0:T(8,128)(2,1)S(1)}, u32[]{:S(2)}, u32[]{:S(2)}) collective-permute-start(bf16[512,512]{1,0:T(8,128)(2,1)} %param.17), channel_id=1, source_target_pairs={{0,1},{1,2},{2,3},{3,0},{4,5},{5,6},{6,7},{7,4},{8,9},{9,10},{10,1... | collective-permute-start | bytes 1572872 | tf_op jit(solution)/shard_map/ppermute | solution.py:16
  1.2 20.9 %collective-permute-start.2 = (bf16[512,512]{1,0:T(8,128)(2,1)}, bf16[512,512]{1,0:T(8,128)(2,1)S(1)}, u32[]{:S(2)}, u32[]{:S(2)}) collective-permute-start(bf16[512,512]{1,0:T(8,128)(2,1)} %param.17), channel_id=1, source_target_pairs={{0,3},{1,0},{2,1},{3,2},{4,7},{5,4},{6,5},{7,6},{8,11},{9,8},{10,9... | collective-permute-start | bytes 1572872 | tf_op jit(solution)/shard_map/ppermute | solution.py:18
  13.2 8.6 %collective-permute-start.1 = (bf16[512,512]{1,0:T(8,128)(2,1)S(1)}, bf16[512,512]{1,0:T(8,128)(2,1)S(1)}, u32[]{:S(2)}, u32[]{:S(2)}) collective-permute-start(bf16[512,512]{1,0:T(8,128)(2,1)S(1)} %collective-permute-done), channel_id=1, source_target_pairs={{0,1},{1,2},{2,3},{3,0},{4,5},{5,6},{6,7},{7,4},{8,9},{9,10},{10,1... | collective-permute-start | bytes 1572872 | tf_op jit(solution)/shard_map/ppermute | solution.py:16
  16.2 5.7 %copy-start.10 = (bf16[512,512]{1,0:T(8,128)(2,1)S(1)}, bf16[512,512]{1,0:T(8,128)(2,1)}, u32[]{:S(2)}) copy-start(bf16[512,512]{1,0:T(8,128)(2,1)} %param.17) | copy-start | bytes 1572868
  22.5 1.0 %copy-start.14 = (bf16[512,256]{1,0:T(8,128)(2,1)S(1)}, bf16[512,256]{1,0:T(8,128)(2,1)}, u32[]{:S(2)}) copy-start(bf16[512,256]{1,0:T(8,128)(2,1)} %param.14) | copy-start | bytes 786436
  22.5 1.3 %copy-start.8 = (bf16[512,256]{1,0:T(8,128)(2,1)S(1)}, bf16[512,256]{1,0:T(8,128)(2,1)}, u32[]{:S(2)}) copy-start(bf16[512,256]{1,0:T(8,128)(2,1)} %param.15) | copy-start | bytes 786436
  22.5 1.3 %copy-start.12 = (bf16[512,256]{1,0:T(8,128)(2,1)S(1)}, bf16[512,256]{1,0:T(8,128)(2,1)}, u32[]{:S(2)}) copy-start(bf16[512,256]{1,0:T(8,128)(2,1)} %param.16) | copy-start | bytes 786436
  22.5 5.4 %copy-start.5 = (f32[512,512]{1,0:T(8,128)S(1)}, f32[512,512]{1,0:T(8,128)}, u32[]{:S(2)}) copy-start(f32[512,512]{1,0:T(8,128)} %get-tuple-element.83) | copy-start | bytes 3145732
  22.5 5.4 %copy-start.6 = (f32[512,512]{1,0:T(8,128)S(1)}, f32[512,512]{1,0:T(8,128)}, u32[]{:S(2)}) copy-start(f32[512,512]{1,0:T(8,128)} %get-tuple-element.80) | copy-start | bytes 3145732
  22.5 5.4 %copy-start.7 = (f32[512,512]{1,0:T(8,128)S(1)}, f32[512,512]{1,0:T(8,128)}, u32[]{:S(2)}) copy-start(f32[512,512]{1,0:T(8,128)} %get-tuple-element.81) | copy-start | bytes 3145732
  23.3 4.6 %copy-start.2 = (f32[512,512]{1,0:T(8,128)S(1)}, f32[512,512]{1,0:T(8,128)}, u32[]{:S(2)}) copy-start(f32[512,512]{1,0:T(8,128)} %get-tuple-element.84) | copy-start | bytes 3145732
  23.3 4.6 %copy-start.3 = (f32[512,512]{1,0:T(8,128)S(1)}, f32[512,512]{1,0:T(8,128)}, u32[]{:S(2)}) copy-start(f32[512,512]{1,0:T(8,128)} %get-tuple-element.85) | copy-start | bytes 3145732
  23.3 4.6 %copy-start.4 = (f32[512,512]{1,0:T(8,128)S(1)}, f32[512,512]{1,0:T(8,128)}, u32[]{:S(2)}) copy-start(f32[512,512]{1,0:T(8,128)} %get-tuple-element.82) | copy-start | bytes 3145732
  24.8 7.6 %collective-permute-start.6 = (f32[2,128,128]{1,2,0:T(8,128)S(1)}, f32[2,128,128]{1,2,0:T(8,128)S(1)}, u32[]{:S(2)}, u32[]{:S(2)}) collective-permute-start(f32[2,128,128]{1,2,0:T(8,128)S(1)} %get-tuple-element.50), channel_id=1, source_target_pairs={{0,16},{4,20},{8,24},{12,28},{16,0},{20,4},{24,8},{28,12},{1,17},{... | collective-permute-start | bytes 393224 | tf_op jit(solution)/shard_map/ppermute | solution.py:24
  29.8 9.6 %collective-permute-start.4 = (f32[2,128,128]{1,2,0:T(8,128)S(1)}, f32[2,128,128]{1,2,0:T(8,128)}, u32[]{:S(2)}, u32[]{:S(2)}) collective-permute-start(f32[2,128,128]{1,2,0:T(8,128)S(1)} %get-tuple-element.51), channel_id=1, source_target_pairs={{0,8},{4,12},{8,0},{12,4},{16,24},{20,28},{24,16},{28,20},{1,9},{5... | collective-permute-start | bytes 393224 | tf_op jit(solution)/shard_map/ppermute | solution.py:24
  32.4 7.9 %collective-permute-start.7 = (f32[2,128,128]{1,2,0:T(8,128)S(1)}, f32[2,128,128]{1,2,0:T(8,128)S(1)}, u32[]{:S(2)}, u32[]{:S(2)}) collective-permute-start(f32[2,128,128]{1,2,0:T(8,128)S(1)} %collective-permute-done.6), channel_id=1, source_target_pairs={{0,4},{4,0},{8,12},{12,8},{16,20},{20,16},{24,28},{28,24},{1,5},{5... | collective-permute-start | bytes 393224 | tf_op jit(solution)/shard_map/ppermute | solution.py:24
  35.5 10.0 %collective-permute-start.3 = (f32[2,128,128]{1,2,0:T(8,128)}, f32[2,128,128]{1,2,0:T(8,128)}, u32[]{:S(2)}, u32[]{:S(2)}) collective-permute-start(f32[2,128,128]{1,2,0:T(8,128)} %get-tuple-element.49), channel_id=1, source_target_pairs={{0,4},{4,0},{8,12},{12,8},{16,20},{20,16},{24,28},{28,24},{1,5},{5... | collective-permute-start | bytes 393224 | tf_op jit(solution)/shard_map/ppermute | solution.py:24
  39.4 8.7 %collective-permute-start.5 = (f32[2,128,128]{1,2,0:T(8,128)}, f32[2,128,128]{1,2,0:T(8,128)}, u32[]{:S(2)}, u32[]{:S(2)}) collective-permute-start(f32[2,128,128]{1,2,0:T(8,128)} %collective-permute-done.4), channel_id=1, source_target_pairs={{0,4},{4,0},{8,12},{12,8},{16,20},{20,16},{24,28},{28,24},{1,5},{5... | collective-permute-start | bytes 393224 | tf_op jit(solution)/shard_map/ppermute | solution.py:24
  40.3 9.1 %collective-permute-start.8 = (f32[2,128,128]{1,2,0:T(8,128)S(1)}, f32[2,128,128]{1,2,0:T(8,128)}, u32[]{:S(2)}, u32[]{:S(2)}) collective-permute-start(f32[2,128,128]{1,2,0:T(8,128)S(1)} %add.537), channel_id=1, source_target_pairs={{0,8},{4,12},{8,0},{12,4},{16,24},{20,28},{24,16},{28,20},{1,9},{5... | collective-permute-start | bytes 393224 | tf_op jit(solution)/shard_map/ppermute | solution.py:24
  45.5 5.5 %copy-start.1 = (bf16[2,512,512]{2,1,0:T(8,128)(2,1)S(1)}, bf16[2,512,512]{2,1,0:T(8,128)(2,1)}, u32[]{:S(2)}) copy-start(bf16[2,512,512]{2,1,0:T(8,128)(2,1)} %multiply_convert_fusion.1) | copy-start | bytes 3145732
  45.5 5.5 %copy-start.9 = (bf16[512,256]{1,0:T(8,128)(2,1)S(1)}, bf16[512,256]{1,0:T(8,128)(2,1)}, u32[]{:S(2)}) copy-start(bf16[512,256]{1,0:T(8,128)(2,1)} %param.15) | copy-start | bytes 786436
  50.6 1.8 %copy-start.13 = (bf16[512,256]{1,0:T(8,128)(2,1)S(1)}, bf16[512,256]{1,0:T(8,128)(2,1)}, u32[]{:S(2)}) copy-start(bf16[512,256]{1,0:T(8,128)(2,1)} %param.16) | copy-start | bytes 786436
  51.5 3.3 %copy-start.11 = (f32[2,128,512]{2,1,0:T(8,128)S(1)}, f32[2,128,512]{2,1,0:T(8,128)}, u32[]{:S(2)}) copy-start(f32[2,128,512]{2,1,0:T(8,128)} %fusion.3) | copy-start | bytes 1572868
